TPU v7x, 32 devices: a whole 2x2x4 slice. The times are simulated.
32 devices in a mesh: front: 4 (over y, core), row: 8 (over z, x).
Axes of the slice: x: 2, y: 2, z: 4, core: 2. Of those that a mesh axis runs over, the one named last changes fastest.
Arguments:
- rhs_diag: float32 [4, 32, 2048], P('front', None, 'row'), may hold values from -6 to 6
- rhs_off: float32 [4, 32, 12288], P('front', None, 'row'), may hold values from -6 to 6
- diag_factor: float32 [4, 2048, 2048], P('front', 'row'), may hold values from -0.125 to 0.125
- off_factor: float32 [4, 12288, 2048], P('front', 'row'), may hold values from -0.125 to 0.125
- diag_inverse: float32 [4, 4, 512, 512], P('front')
- pattern: int32 [4, 4, 96], P('front', None, 'row'), may hold values 0 or 1
- upd_vals: float32 [32, 4, 8, 4, 8, 128], P(None, 'front', 'row'), may hold values from -4 to 4
- upd_rows: int32 [4, 8, 4, 8, 128], P('front', 'row'), may hold values from 0 to 1791
Outputs:
- solved: float32 [4, 32, 2048], P('front', None, 'row')
- remainder: float32 [4, 32, 12288], P('front', None, 'row')
Inputs may be any that keep to these rules, and one draw needn't show every extreme that they name: `upd_rows`: relative rows of the receiving row block: below 256 a window row, else a row below the window; several entries may name one row.
All inputs are finite; a program needn't handle non-finite values. No bound on the sum of `pattern` on one device may be relied on, other than what follows from the above.
Results may differ from a plain program's by a relative error of at most 0.0001.
Values sent between devices are 32-bit elements; how exact they have to be, the bound alone decides.
A program may use at most 128 MiB of HBM per device.

v0:
```python
import functools

import jax
import jax.numpy as jnp
from jax import lax
from jax.experimental import pallas as pl
from jax.experimental.pallas import tpu as pltpu
from jax.sharding import PartitionSpec as P

W = 512
BR = 128
MESH = pl.DeviceIdType.MESH
PART = 256
NT = (((1,), (1,)), ((), ()))


def split(x):
    hi = x.astype(jnp.bfloat16)
    lo = (x - hi.astype(jnp.float32)).astype(jnp.bfloat16)
    return hi, lo


def dot_nt(a, b):
    return lax.dot_general(a, b, NT, preferred_element_type=jnp.float32)


def dot3(a2, b_hi, b_lo):
    n = a2.shape[0] // 2
    top = dot_nt(a2, b_hi)
    return top[:n] + top[n:] + dot_nt(a2[:n], b_lo)


def kernel(nf, nr, rd_ref, ro_ref, diag_hbm, off_hbm, inv_hbm, pat_ref, vals_hbm, rows_ref,
           solved_ref, rem_ref,
           diag_f, off_f, inv_f, diag_h, diag_l, off_h, off_l, inv_h, inv_l,
           recv, vs, hot, code_ref, low_acc, upper, rhsbuf, load_sem, own_sem, a2a_send, a2a_recv, pan_send, pan_recv):
    f = lax.axis_index("front")
    r = lax.axis_index("row")
    devices = nf * nr
    nrhs, rd = upper.shape
    od = off_f.shape[0]
    panels = inv_f.shape[0]
    per = W // rd
    slot = recv.shape[3]

    load_inv = pltpu.make_async_copy(inv_hbm.at[0], inv_f, load_sem.at[0])
    load_diag = pltpu.make_async_copy(diag_hbm.at[0], diag_f, load_sem.at[1])
    load_off = pltpu.make_async_copy(off_hbm.at[0], off_f, load_sem.at[2])

    def peer(d):
        return lax.rem(f + d // nr, nf), lax.rem(r + lax.rem(d, nr), nr)

    barrier = pltpu.get_barrier_semaphore()

    def greet(d, c):
        pf, pr = peer(d)
        pl.semaphore_signal(barrier, inc=1, device_id=(pf, pr), device_id_type=MESH)
        return c

    lax.fori_loop(1, devices, greet, 0)
    load_inv.start()
    load_diag.start()
    load_off.start()
    own = pltpu.make_async_copy(vals_hbm.at[:, f, r, :], recv.at[f, r], own_sem)
    own.start()
    pl.semaphore_wait(barrier, devices - 1)

    def exchange(d):
        pf, pr = peer(d)
        return pltpu.make_async_remote_copy(
            src_ref=vals_hbm.at[:, pf, pr, :],
            dst_ref=recv.at[f, r],
            send_sem=a2a_send.at[d],
            recv_sem=a2a_recv.at[d],
            device_id=(pf, pr),
            device_id_type=MESH,
        )

    def send(d, c):
        exchange(d).start()
        return c

    lax.fori_loop(1, devices, send, 0)

    code_ref[...] = rows_ref[...] + (PART - rd)

    def mark(s, c):
        low = code_ref[pl.ds(s, 1), :] & (PART - 1)
        ids = lax.broadcasted_iota(jnp.int32, (PART, slot), 0)
        at = pl.ds(pl.multiple_of(s * slot, slot), slot)
        hot[:, at] = jnp.where(low == ids, 1.0, 0.0).astype(jnp.bfloat16)
        return c

    lax.fori_loop(0, devices, mark, 0)

    load_inv.wait()
    for p in range(panels):
        def split_inv(i, c, p=p):
            at = pl.ds(pl.multiple_of(i * 64, 64), 64)
            hi, lo = split(inv_f[p, at, :])
            inv_h[p, at, :] = hi
            inv_l[p, at, :] = lo
            return c

        lax.fori_loop(0, W // 64, split_inv, 0)
    load_diag.wait()

    def split_diag(i, c):
        at = pl.ds(pl.multiple_of(i * 16, 16), 16)
        hi, lo = split(diag_f[at, :])
        diag_h[at, :] = hi
        diag_l[at, :] = lo
        return c

    lax.fori_loop(0, rd // 16, split_diag, 0)
    load_off.wait()

    def split_off(i, c):
        at = pl.ds(pl.multiple_of(i * 16, 16), 16)
        hi, lo = split(off_f[at, :])
        off_h[at, :] = hi
        off_l[at, :] = lo
        return c

    lax.fori_loop(0, od // 16, split_off, 0)

    own.wait()

    def arrive(d, c):
        exchange(d).wait_recv()
        return c

    lax.fori_loop(1, devices, arrive, 0)

    for sf in range(nf):
        def split_vals(sr, c, sf=sf):
            hi, lo = split(recv[sf, sr])
            at = pl.ds(pl.multiple_of((sf * nr + sr) * slot, slot), slot)
            vs[pl.ds(0, nrhs), at] = hi
            vs[pl.ds(nrhs, nrhs), at] = lo
            return c

        lax.fori_loop(0, nr, split_vals, 0)

    group = 4
    span = group * slot

    def picked(k, parts):
        block = code_ref[pl.ds(k * group, group), :]
        part = jnp.concatenate([block[g:g + 1, :] for g in range(group)], axis=1) >> 8
        values = vs[:, pl.ds(pl.multiple_of(k * span, span), span)]
        rows = []
        for h in parts:
            mask = jnp.where(jnp.broadcast_to(part, (16, span)) == h, 1.0, 0.0).astype(jnp.bfloat16)
            rows.append(values * jnp.concatenate([mask] * (2 * nrhs // 16), axis=0))
        return jnp.concatenate(rows, axis=0)

    def reduced(acc, h):
        return acc[2 * h * nrhs:(2 * h + 1) * nrhs] + acc[(2 * h + 1) * nrhs:(2 * h + 2) * nrhs]

    steps = devices // group
    unroll = 8

    def upper_step(i, acc):
        for u in range(unroll):
            k = i * unroll + u
            acc = acc + dot_nt(picked(k, [0]), hot[:, pl.ds(pl.multiple_of(k * span, span), span)])
        return acc

    acc = lax.fori_loop(0, steps // unroll, upper_step, jnp.zeros((2 * nrhs, PART), jnp.float32))
    upper[...] = rd_ref[0] + reduced(acc, 0)[:, PART - rd:]

    chunk = 2 * BR
    chunks = od // chunk
    parts = list(range(1, chunks + 1))

    def scatter_lower():
        low_acc[...] = jnp.zeros_like(low_acc)

        def step(k, c):
            low_acc[...] += dot_nt(picked(k, parts), hot[:, pl.ds(pl.multiple_of(k * span, span), span)])
            return c

        lax.fori_loop(0, steps, step, 0)
        for h in range(chunks):
            at = pl.ds(h * chunk, chunk)
            rem_ref[0, :, at] = ro_ref[0, :, at] + reduced(low_acc, h)

    def off_update(p, piece2):
        def step(i, c):
            at = pl.ds(pl.multiple_of(i * chunk, chunk), chunk)
            columns = pl.ds(p * W, W)
            term = dot3(piece2, off_h[at, columns], off_l[at, columns])
            scaled = jnp.concatenate(
                [term[:, b * BR:(b + 1) * BR] * pat_ref[0, p, 2 * i + b].astype(jnp.float32) for b in range(2)], axis=1)
            rem_ref[0, :, at] -= scaled
            return c

        lax.fori_loop(0, chunks, step, 0)

    def share(d):
        return pltpu.make_async_remote_copy(
            src_ref=rhsbuf.at[r],
            dst_ref=rhsbuf.at[r],
            send_sem=pan_send.at[d],
            recv_sem=pan_recv.at[r],
            device_id=(f, lax.rem(r + d, nr)),
            device_id_type=MESH,
        )

    piece2 = None
    for p in range(panels):
        @pl.when(r // per == p)
        def _():
            rhsbuf[r] = upper[...]

            def start(d, c):
                share(d).start()
                return c

            lax.fori_loop(1, nr, start, 0)

        if p == 0:
            scatter_lower()
        else:
            off_update(p - 1, piece2)

        for j in range(p * per, (p + 1) * per):
            @pl.when(r != j)
            def _(j=j):
                pltpu.make_async_remote_copy(
                    src_ref=rhsbuf.at[j],
                    dst_ref=rhsbuf.at[j],
                    send_sem=pan_send.at[0],
                    recv_sem=pan_recv.at[j],
                    device_id=(f, j),
                    device_id_type=MESH,
                ).wait_recv()

        panel_rhs = jnp.concatenate([rhsbuf[j] for j in range(p * per, (p + 1) * per)], axis=1)
        piece = dot3(jnp.concatenate(split(panel_rhs), axis=0), inv_h[p], inv_l[p])
        piece2 = jnp.concatenate(split(piece), axis=0)
        if p < panels - 1:
            @pl.when(r // per > p)
            def _(piece2=piece2, p=p):
                columns = pl.ds(p * W, W)
                upper[...] -= dot3(piece2, diag_h[:, columns], diag_l[:, columns])

        for i in range(per):
            @pl.when(r == p * per + i)
            def _(i=i, piece=piece):
                solved_ref[0] = piece[:, i * rd:(i + 1) * rd]

    off_update(panels - 1, piece2)

    def sent(d, c):
        exchange(d).wait_send()
        return c

    lax.fori_loop(1, devices, sent, 0)

    def shared(d, c):
        share(d).wait_send()
        return c

    lax.fori_loop(1, nr, shared, 0)


def local(nf, nr, rhs_diag, rhs_off, diag_factor, off_factor, diag_inverse, pattern, upd_vals, upd_rows):
    nrhs = upd_vals.shape[0]
    slot = upd_vals.shape[5]
    rd = diag_factor.shape[1]
    od = off_factor.shape[1]
    k = diag_factor.shape[2]
    panels = diag_inverse.shape[1]
    devices = nf * nr
    vals = upd_vals.reshape(upd_vals.shape[0], nf, nr, slot)
    rows = upd_rows.reshape(devices, slot)
    vmem = pl.BlockSpec(memory_space=pltpu.VMEM)
    anywhere = pl.BlockSpec(memory_space=pl.ANY)
    f32, bf16 = jnp.float32, jnp.bfloat16
    return pl.pallas_call(
        functools.partial(kernel, nf, nr),
        out_shape=(
            jax.ShapeDtypeStruct((1, nrhs, rd), f32),
            jax.ShapeDtypeStruct((1, nrhs, od), f32),
        ),
        in_specs=[vmem, vmem, anywhere, anywhere, anywhere,
                  pl.BlockSpec(memory_space=pltpu.SMEM), anywhere, vmem],
        out_specs=(vmem, vmem),
        scratch_shapes=[
            pltpu.VMEM((rd, k), f32),
            pltpu.VMEM((od, k), f32),
            pltpu.VMEM((panels, W, W), f32),
            pltpu.VMEM((rd, k), bf16),
            pltpu.VMEM((rd, k), bf16),
            pltpu.VMEM((od, k), bf16),
            pltpu.VMEM((od, k), bf16),
            pltpu.VMEM((panels, W, W), bf16),
            pltpu.VMEM((panels, W, W), bf16),
            pltpu.VMEM((nf, nr, nrhs, slot), f32),
            pltpu.VMEM((2 * nrhs, devices * slot), bf16),
            pltpu.VMEM((PART, devices * slot), bf16),
            pltpu.VMEM((devices, slot), jnp.int32),
            pltpu.VMEM((2 * nrhs * od // PART, PART), f32),
            pltpu.VMEM((nrhs, rd), f32),
            pltpu.VMEM((nr, nrhs, rd), f32),
            pltpu.SemaphoreType.DMA((3,)),
            pltpu.SemaphoreType.DMA,
            pltpu.SemaphoreType.DMA((devices,)),
            pltpu.SemaphoreType.DMA((devices,)),
            pltpu.SemaphoreType.DMA((nr,)),
            pltpu.SemaphoreType.DMA((nr,)),
        ],
        compiler_params=pltpu.CompilerParams(
            collective_id=0, has_side_effects=True, vmem_limit_bytes=58 * 1024 * 1024),
    )(rhs_diag, rhs_off, diag_factor, off_factor, diag_inverse, pattern, vals, rows)


def solution(mesh):
    in_specs = (
        P("front", None, "row"),
        P("front", None, "row"),
        P("front", "row", None),
        P("front", "row", None),
        P("front", None, None, None),
        P("front", None, "row"),
        P(None, "front", "row", None, None, None),
        P("front", "row", None, None, None),
    )
    out_specs = (P("front", None, "row"), P("front", None, "row"))
    body = functools.partial(local, mesh.shape["front"], mesh.shape["row"])
    return jax.shard_map(body, mesh=mesh, in_specs=in_specs, out_specs=out_specs, check_vma=False)
```

profile of v0, /device:TPU:0, one launch (start us, length us, event | category | flops | bytes accessed | tf_op | source)
XLA Modules:
  0.0 47.5 jit_solution(6204753464475210070)
XLA Ops:
  0.6 43.9 %shard_map.95 = (f32[1,32,256]{2,1,0:T(8,128)}, f32[1,32,1536]{2,1,0:T(8,128)}) custom-call(f32[1,32,256]{2,1,0:T(8,128)} %rd_ref.1, f32[1,32,1536]{2,1,0:T(8,128)} %ro_ref.1, f32[1,256,2048]{2,1,0:T(8,128)} %diag_hbm.1, f32[1,1536,2048]{2,1,0:T(8,128)} %off_hbm.1, f32[1,4,512,512]{3,2,1,0:T(8,128)} %inv_hbm.1, s32[1,4,12]{2,1,0:T(4,128)} %pat_ref.1, ...), custom_call_target="tpu_custom_call" | custom-call | tf_op jit(solution)/shard_map/pallas_call | solution.py:282
  44.5 1.4 %copy.12 = f32[1,32,256]{2,1,0:T(8,128)} copy(f32[1,32,256]{2,1,0:T(8,128)} %get-tuple-element.4) | data formatting | bytes 65536
  45.9 1.6 %copy.13 = f32[1,32,1536]{2,1,0:T(8,128)} copy(f32[1,32,1536]{2,1,0:T(8,128)} %get-tuple-element.5) | data formatting | bytes 393216
where the time goes:
time: 47.8 us; the launch traced here: 47.5 us
  Pallas kernels  43.9 us (92%)
  local copies, waits for them, and re-layouts  2.99 us (6%)
  between operations  0.64 us (1%)
    pallas_call x1, Pallas kernels, local(): pl.pallas_call(functools.partial(kernel, nf, nr), out_shape=(jax.ShapeDty...  43.9 us
    unnamed x2, local copies, waits for them, and re-layouts  2.99 us

commit v1 on v0

v1 whole, which is shorter than its diff:
```python
import functools

import jax
import jax.numpy as jnp
from jax import lax
from jax.experimental import pallas as pl
from jax.experimental.pallas import tpu as pltpu
from jax.sharding import PartitionSpec as P

W = 512
BR = 128
MESH = pl.DeviceIdType.MESH
PART = 256
NT = (((1,), (1,)), ((), ()))


def split(x):
    hi = x.astype(jnp.bfloat16)
    lo = (x - hi.astype(jnp.float32)).astype(jnp.bfloat16)
    return hi, lo


def dot_nt(a, b):
    return lax.dot_general(a, b, NT, preferred_element_type=jnp.float32)


def dot3(a2, b_hi, b_lo):
    n = a2.shape[0] // 2
    top = dot_nt(a2, b_hi)
    return top[:n] + top[n:] + dot_nt(a2[:n], b_lo)


def reach(planes, plane):
    orders = [sorted(range(planes), key=lambda q, z=z: (abs(q - z), q)) for z in range(planes)]
    out = []
    for i in range(planes):
        q = jnp.int32(orders[0][i])
        for z in range(1, planes):
            q = jnp.where(plane == z, jnp.int32(orders[z][i]), q)
        out.append(q)
    return out


def kernel(nf, nr, rd_hbm, ro_hbm, diag_hbm, off_hbm, inv_hbm, pat_hbm, vals_hbm, rows_hbm,
           solved_ref, rem_ref,
           diag_f, off_f, inv_f, diag_h, diag_l, off_h, off_l, inv_h, inv_l, step_h, step_l,
           recv, vs, hot, rows_v, code_ref, acc, upper, rhsbuf, rd_v, ro_v, pat_ref,
           load_sem, own_sem, a2a_send, a2a_recv, pan_send, pan_recv):
    f = lax.axis_index("front")
    r = lax.axis_index("row")
    devices = nf * nr
    nrhs, rd = upper.shape
    od = off_f.shape[0]
    panels = inv_f.shape[0]
    per = W // rd
    slot = recv.shape[3]
    members = nf * per
    plane = r // per
    place = lax.rem(r, per)
    me = f * nr + r

    barrier = pltpu.get_barrier_semaphore()

    def greet(d, c):
        pf = lax.rem(f + d // nr, nf)
        pr = lax.rem(r + lax.rem(d, nr), nr)
        pl.semaphore_signal(barrier, inc=1, device_id=(pf, pr), device_id_type=MESH)
        return c

    lax.fori_loop(1, devices, greet, 0)

    load_rows = pltpu.make_async_copy(rows_hbm, rows_v, load_sem.at[0])
    load_inv = pltpu.make_async_copy(inv_hbm.at[0], inv_f, load_sem.at[1])
    load_diag = pltpu.make_async_copy(diag_hbm.at[0], diag_f, load_sem.at[2])
    load_off = pltpu.make_async_copy(off_hbm.at[0], off_f, load_sem.at[3])
    load_rd = pltpu.make_async_copy(rd_hbm.at[0], rd_v, load_sem.at[4])
    load_ro = pltpu.make_async_copy(ro_hbm.at[0], ro_v, load_sem.at[5])
    load_pat = pltpu.make_async_copy(pat_hbm.at[0], pat_ref, load_sem.at[6])
    own = pltpu.make_async_copy(vals_hbm.at[:, f, r, :], recv.at[f, r], own_sem)
    for load in (load_rows, load_inv, load_diag, load_off, load_rd, load_ro, load_pat, own):
        load.start()

    def exchange(pf, pr, source):
        return pltpu.make_async_remote_copy(
            src_ref=vals_hbm.at[:, pf, pr, :],
            dst_ref=recv.at[source // nr, lax.rem(source, nr)],
            send_sem=a2a_send.at[pf * nr + pr],
            recv_sem=a2a_recv.at[source],
            device_id=(pf, pr),
            device_id_type=MESH,
        )

    pl.semaphore_wait(barrier, devices - 1)

    def target(t):
        i = lax.rem(t, members)
        pf = lax.rem(f + i // per, nf)
        pr = (t // members) * per + lax.rem(place + i, per)
        return pf, pr

    def send(t, c):
        pf, pr = target(t)

        @pl.when(pf * nr + pr != me)
        def _():
            exchange(pf, pr, me).start()

        return c

    lax.fori_loop(0, devices, send, 0)

    def source_of(s):
        i = lax.rem(s, members)
        return i // per, (s // members) * per + lax.rem(i, per)

    load_rows.wait()

    def mark(s, c):
        sf, sr = source_of(s)
        code = rows_v[pl.ds(sf * nr + sr, 1), :] + (PART - rd)
        code_ref[pl.ds(s, 1), :] = code
        ids = lax.broadcasted_iota(jnp.int32, (PART, slot), 0)
        at = pl.ds(pl.multiple_of(s * slot, slot), slot)
        hot[:, at] = jnp.where((code & (PART - 1)) == ids, 1.0, 0.0).astype(jnp.bfloat16)
        return c

    lax.fori_loop(0, devices, mark, 0)

    load_inv.wait()
    for p in range(panels):
        def split_inv(i, c, p=p):
            at = pl.ds(pl.multiple_of(i * 64, 64), 64)
            hi, lo = split(inv_f[p, at, :])
            inv_h[p, at, :] = hi
            inv_l[p, at, :] = lo
            return c

        lax.fori_loop(0, W // 64, split_inv, 0)
    load_diag.wait()

    def split_diag(i, c):
        at = pl.ds(pl.multiple_of(i * 16, 16), 16)
        hi, lo = split(diag_f[at, :])
        diag_h[at, :] = hi
        diag_l[at, :] = lo
        return c

    lax.fori_loop(0, rd // 16, split_diag, 0)

    for p in range(panels - 1):
        @pl.when(plane > p)
        def _(p=p):
            for n in range(2):
                columns = pl.ds(n * (W // 2), W // 2)
                left_h = diag_h[:, pl.ds(p * W, W)]
                left_l = diag_l[:, pl.ds(p * W, W)]
                right_h = inv_h[p, :, columns]
                product = (jnp.dot(left_h, right_h, preferred_element_type=jnp.float32)
                           + jnp.dot(left_l, right_h, preferred_element_type=jnp.float32)
                           + jnp.dot(left_h, inv_l[p, :, columns], preferred_element_type=jnp.float32))
                hi, lo = split(product)
                step_h[p, :, columns] = hi
                step_l[p, :, columns] = lo

    load_off.wait()

    def split_off(i, c):
        at = pl.ds(pl.multiple_of(i * 16, 16), 16)
        hi, lo = split(off_f[at, :])
        off_h[at, :] = hi
        off_l[at, :] = lo
        return c

    lax.fori_loop(0, od // 16, split_off, 0)

    group = 4
    span = group * slot
    per_plane = members // group
    chunk = 2 * BR
    chunks = od // chunk
    lower_parts = list(range(1, chunks + 1))

    def columns_of(g):
        return pl.ds(pl.multiple_of(g * span, span), span)

    def picked(g, parts):
        block = code_ref[pl.ds(pl.multiple_of(g * group, group), group), :]
        part = jnp.concatenate([block[u:u + 1, :] for u in range(group)], axis=1) >> 8
        values = vs[:, columns_of(g)]
        rows = []
        for h in parts:
            mask = jnp.where(jnp.broadcast_to(part, (16, span)) == h, 1.0, 0.0).astype(jnp.bfloat16)
            rows.append(values * jnp.concatenate([mask] * (2 * nrhs // 16), axis=0))
        return jnp.concatenate(rows, axis=0)

    def take(g):
        for u in range(group):
            s = g * group + u
            sf, sr = source_of(s)

            @pl.when(sf * nr + sr != me)
            def _(sf=sf, sr=sr):
                exchange(sf, sr, sf * nr + sr).wait_recv()

            hi, lo = split(recv[sf, sr])
            at = pl.ds(pl.multiple_of(s * slot, slot), slot)
            vs[pl.ds(0, nrhs), at] = hi
            vs[pl.ds(nrhs, nrhs), at] = lo

    upper_rows = pl.ds(0, 2 * nrhs)
    lower_rows = pl.ds(2 * nrhs, 2 * nrhs * chunks)

    def add_all(g):
        acc[...] += dot_nt(picked(g, [0] + lower_parts), hot[:, columns_of(g)])

    def add_upper(g):
        acc[upper_rows, :] += dot_nt(picked(g, [0]), hot[:, columns_of(g)])

    def add_lower(g):
        acc[lower_rows, :] += dot_nt(picked(g, lower_parts), hot[:, columns_of(g)])

    def reduced(h):
        at = 2 * h * nrhs
        return acc[at:at + nrhs, :] + acc[at + nrhs:at + 2 * nrhs, :]

    acc[...] = jnp.zeros_like(acc)
    load_rd.wait()
    load_ro.wait()
    load_pat.wait()
    own.wait()
    order = reach(panels, plane)
    for q in order[:-1]:
        def near(i, c, q=q):
            g = q * per_plane + i
            take(g)
            add_all(g)
            return c

        lax.fori_loop(0, per_plane, near, 0)

    def far(i, c):
        g = order[-1] * per_plane + i
        take(g)
        add_upper(g)
        return c

    lax.fori_loop(0, per_plane, far, 0)
    upper[...] = rd_v[...] + reduced(0)[:, PART - rd:]

    def scatter_lower():
        def step(i, c):
            add_lower(order[-1] * per_plane + i)
            return c

        lax.fori_loop(0, per_plane, step, 0)
        for h in range(chunks):
            at = pl.ds(h * chunk, chunk)
            rem_ref[0, :, at] = ro_v[:, at] + reduced(h + 1)

    def off_update(p, piece2):
        def step(i, c):
            at = pl.ds(pl.multiple_of(i * chunk, chunk), chunk)
            columns = pl.ds(p * W, W)
            term = dot3(piece2, off_h[at, columns], off_l[at, columns])
            scaled = jnp.concatenate(
                [term[:, b * BR:(b + 1) * BR] * pat_ref[p, 2 * i + b].astype(jnp.float32) for b in range(2)], axis=1)
            rem_ref[0, :, at] -= scaled
            return c

        lax.fori_loop(0, chunks, step, 0)

    def share(to, j):
        return pltpu.make_async_remote_copy(
            src_ref=rhsbuf.at[j],
            dst_ref=rhsbuf.at[j],
            send_sem=pan_send.at[to],
            recv_sem=pan_recv.at[j],
            device_id=(f, to),
            device_id_type=MESH,
        )

    def finish(p, b2):
        piece = dot3(b2, inv_h[p], inv_l[p])
        for i in range(per):
            @pl.when(r == p * per + i)
            def _(i=i):
                solved_ref[0] = piece[:, i * rd:(i + 1) * rd]
        off_update(p, jnp.concatenate(split(piece), axis=0))

    b2 = None
    for p in range(panels):
        @pl.when(plane == p)
        def _(p=p):
            rhsbuf[r] = upper[...]
            if p < panels - 1:
                targets = [(p + 1) * per + lax.rem(place + i, per) for i in range(per)]
                targets += [p * per + lax.rem(place + i, per) for i in range(1, per)]
                targets += [q * per + lax.rem(place + i, per)
                            for q in [*range(p + 2, panels), *range(p - 1, -1, -1)] for i in range(per)]
            else:
                targets = [q * per + i for q in range(panels - 1) for i in range(per)]
                targets += [p * per + lax.rem(place + i, per) for i in range(1, per)]
            for to in targets:
                share(to, r).start()

        if p == 0:
            scatter_lower()
        else:
            finish(p - 1, b2)

        for j in range(p * per, (p + 1) * per):
            @pl.when(r != j)
            def _(j=j):
                share(j, j).wait_recv()

        b = jnp.concatenate([rhsbuf[j] for j in range(p * per, (p + 1) * per)], axis=1)
        b2 = jnp.concatenate(split(b), axis=0)
        if p < panels - 1:
            @pl.when(plane > p)
            def _(b2=b2, p=p):
                upper[...] -= dot3(b2, step_h[p], step_l[p])

    finish(panels - 1, b2)

    def sent(t, c):
        pf, pr = target(t)

        @pl.when(pf * nr + pr != me)
        def _():
            exchange(pf, pr, me).wait_send()

        return c

    lax.fori_loop(0, devices, sent, 0)

    def shared(d, c):
        share(lax.rem(r + d, nr), r).wait_send()
        return c

    lax.fori_loop(1, nr, shared, 0)


def hand_out(solved_in, rem_in, solved_out, rem_out):
    solved_out[...] = solved_in[...]
    rem_out[...] = rem_in[...]


def local(nf, nr, rhs_diag, rhs_off, diag_factor, off_factor, diag_inverse, pattern, upd_vals, upd_rows):
    nrhs = upd_vals.shape[0]
    slot = upd_vals.shape[5]
    rd = diag_factor.shape[1]
    od = off_factor.shape[1]
    k = diag_factor.shape[2]
    panels = diag_inverse.shape[1]
    devices = nf * nr
    parts = od // PART + 1
    vals = upd_vals.reshape(upd_vals.shape[0], nf, nr, slot)
    rows = upd_rows.reshape(devices, slot)
    vmem = pl.BlockSpec(memory_space=pltpu.VMEM)
    anywhere = pl.BlockSpec(memory_space=pl.ANY)
    f32, bf16 = jnp.float32, jnp.bfloat16
    outs = (
        jax.ShapeDtypeStruct((1, nrhs, rd), f32),
        jax.ShapeDtypeStruct((1, nrhs, od), f32),
    )
    results = pl.pallas_call(
        functools.partial(kernel, nf, nr),
        out_shape=outs,
        in_specs=[anywhere] * 8,
        out_specs=(vmem, vmem),
        scratch_shapes=[
            pltpu.VMEM((rd, k), f32),
            pltpu.VMEM((od, k), f32),
            pltpu.VMEM((panels, W, W), f32),
            pltpu.VMEM((rd, k), bf16),
            pltpu.VMEM((rd, k), bf16),
            pltpu.VMEM((od, k), bf16),
            pltpu.VMEM((od, k), bf16),
            pltpu.VMEM((panels, W, W), bf16),
            pltpu.VMEM((panels, W, W), bf16),
            pltpu.VMEM((panels - 1, rd, W), bf16),
            pltpu.VMEM((panels - 1, rd, W), bf16),
            pltpu.VMEM((nf, nr, nrhs, slot), f32),
            pltpu.VMEM((2 * nrhs, devices * slot), bf16),
            pltpu.VMEM((PART, devices * slot), bf16),
            pltpu.VMEM((devices, slot), jnp.int32),
            pltpu.VMEM((devices, slot), jnp.int32),
            pltpu.VMEM((2 * nrhs * parts, PART), f32),
            pltpu.VMEM((nrhs, rd), f32),
            pltpu.VMEM((nr, nrhs, rd), f32),
            pltpu.VMEM((nrhs, rd), f32),
            pltpu.VMEM((nrhs, od), f32),
            pltpu.SMEM(pattern.shape[1:], jnp.int32),
            pltpu.SemaphoreType.DMA((7,)),
            pltpu.SemaphoreType.DMA,
            pltpu.SemaphoreType.DMA((devices,)),
            pltpu.SemaphoreType.DMA((devices,)),
            pltpu.SemaphoreType.DMA((nr,)),
            pltpu.SemaphoreType.DMA((nr,)),
        ],
        compiler_params=pltpu.CompilerParams(
            collective_id=0, has_side_effects=True, vmem_limit_bytes=58 * 1024 * 1024),
    )(rhs_diag, rhs_off, diag_factor, off_factor, diag_inverse, pattern, vals, rows)
    return pl.pallas_call(hand_out, out_shape=outs, in_specs=[vmem, vmem], out_specs=(vmem, vmem))(*results)


def solution(mesh):
    in_specs = (
        P("front", None, "row"),
        P("front", None, "row"),
        P("front", "row", None),
        P("front", "row", None),
        P("front", None, None, None),
        P("front", None, "row"),
        P(None, "front", "row", None, None, None),
        P("front", "row", None, None, None),
    )
    out_specs = (P("front", None, "row"), P("front", None, "row"))
    body = functools.partial(local, mesh.shape["front"], mesh.shape["row"])
    return jax.shard_map(body, mesh=mesh, in_specs=in_specs, out_specs=out_specs, check_vma=False)
```

time: 47.8 us -> 43.2 us (0.904)
  local copies, waits for them, and re-layouts: 2.99 us -> 0 us
  Pallas kernels: 43.9 us -> 42.4 us
    unnamed x2 -> x0, local copies, waits for them, and re-layouts: 2.99 us -> none
    pallas_call x1 -> x2, Pallas kernels: 43.9 us -> 42.4 us  [the longest x1 40.8 us: local(): pl.pallas_call(functools.partial(kernel, nf, nr), out_shape=outs, in_spec...]
where the time goes in v1:
time: 43.2 us; the launch traced here: 43.1 us
  Pallas kernels  42.4 us (98%)
  between operations  0.64 us (1%)
    pallas_call x1, Pallas kernels, local(): pl.pallas_call(functools.partial(kernel, nf, nr), out_shape=outs, in_spec...  40.8 us
    pallas_call x1, Pallas kernels, local(): pl.pallas_call(hand_out, out_shape=outs, in_specs=[vmem, vmem], out_specs...  1.64 us

profile of v1, /device:TPU:0, one launch (start us, length us, event | category | flops | bytes accessed | tf_op | source)
XLA Modules:
  0.0 43.1 jit_solution(8554990387207463338)
XLA Ops:
  0.6 40.8 %shard_map.95 = (f32[1,32,256]{2,1,0:T(8,128)}, f32[1,32,1536]{2,1,0:T(8,128)}) custom-call(f32[1,32,256]{2,1,0:T(8,128)} %rd_hbm.1, f32[1,32,1536]{2,1,0:T(8,128)} %ro_hbm.1, f32[1,256,2048]{2,1,0:T(8,128)} %diag_hbm.1, f32[1,1536,2048]{2,1,0:T(8,128)} %off_hbm.1, f32[1,4,512,512]{3,2,1,0:T(8,128)} %inv_hbm.1, s32[1,4,12]{2,1,0:T(4,128)} %pat_hbm.1, ...), custom_call_target="tpu_custom_call" | custom-call | tf_op jit(solution)/shard_map/pallas_call | solution.py:366
  41.4 1.6 %shard_map.96 = (f32[1,32,256]{2,1,0:T(8,128)}, f32[1,32,1536]{2,1,0:T(8,128)}) custom-call(f32[1,32,256]{2,1,0:T(8,128)} %get-tuple-element.4.solved_in, f32[1,32,1536]{2,1,0:T(8,128)} %get-tuple-element.5.rem_in), custom_call_target="tpu_custom_call" | custom-call | tf_op jit(solution)/shard_map/pallas_call | solution.py:404

commit v2 on v1

--- a/solution.py
+++ b/solution.py
@@ -11,6 +11,7 @@
 BR = 128
 MESH = pl.DeviceIdType.MESH
 PART = 256
+CUTS = 1
 NT = (((1,), (1,)), ((), ()))
 
 
@@ -90,6 +91,74 @@
             device_id_type=MESH,
         )
 
+    def source_of(s):
+        i = lax.rem(s, members)
+        return i // per, (s // members) * per + lax.rem(i, per)
+
+    def prepare():
+        load_rows.wait()
+
+        def mark(s, c):
+            sf, sr = source_of(s)
+            code = rows_v[pl.ds(sf * nr + sr, 1), :] + (PART - rd)
+            code_ref[pl.ds(s, 1), :] = code
+            ids = lax.broadcasted_iota(jnp.int32, (PART, slot), 0)
+            at = pl.ds(pl.multiple_of(s * slot, slot), slot)
+            hot[:, at] = jnp.where((code & (PART - 1)) == ids, 1.0, 0.0).astype(jnp.bfloat16)
+            return c
+
+        lax.fori_loop(0, devices, mark, 0)
+
+        load_inv.wait()
+        for p in range(panels):
+            def split_inv(i, c, p=p):
+                at = pl.ds(pl.multiple_of(i * 64, 64), 64)
+                hi, lo = split(inv_f[p, at, :])
+                inv_h[p, at, :] = hi
+                inv_l[p, at, :] = lo
+                return c
+
+            lax.fori_loop(0, W // 64, split_inv, 0)
+        load_diag.wait()
+
+        def split_diag(i, c):
+            at = pl.ds(pl.multiple_of(i * 16, 16), 16)
+            hi, lo = split(diag_f[at, :])
+            diag_h[at, :] = hi
+            diag_l[at, :] = lo
+            return c
+
+        lax.fori_loop(0, rd // 16, split_diag, 0)
+
+        for p in range(panels - 1):
+            @pl.when(plane > p)
+            def _(p=p):
+                for n in range(2):
+                    columns = pl.ds(n * (W // 2), W // 2)
+                    left_h = diag_h[:, pl.ds(p * W, W)]
+                    left_l = diag_l[:, pl.ds(p * W, W)]
+                    right_h = inv_h[p, :, columns]
+                    product = (jnp.dot(left_h, right_h, preferred_element_type=jnp.float32)
+                               + jnp.dot(left_l, right_h, preferred_element_type=jnp.float32)
+                               + jnp.dot(left_h, inv_l[p, :, columns], preferred_element_type=jnp.float32))
+                    hi, lo = split(product)
+                    step_h[p, :, columns] = hi
+                    step_l[p, :, columns] = lo
+
+    def split_lower():
+        load_off.wait()
+
+        def split_off(i, c):
+            at = pl.ds(pl.multiple_of(i * 16, 16), 16)
+            hi, lo = split(off_f[at, :])
+            off_h[at, :] = hi
+            off_l[at, :] = lo
+            return c
+
+        lax.fori_loop(0, od // 16, split_off, 0)
+
+    early = plane < panels // 2
+    pl.when(early)(prepare)
     pl.semaphore_wait(barrier, devices - 1)
 
     def target(t):
@@ -109,69 +178,8 @@
 
     lax.fori_loop(0, devices, send, 0)
 
-    def source_of(s):
-        i = lax.rem(s, members)
-        return i // per, (s // members) * per + lax.rem(i, per)
-
-    load_rows.wait()
-
-    def mark(s, c):
-        sf, sr = source_of(s)
-        code = rows_v[pl.ds(sf * nr + sr, 1), :] + (PART - rd)
-        code_ref[pl.ds(s, 1), :] = code
-        ids = lax.broadcasted_iota(jnp.int32, (PART, slot), 0)
-        at = pl.ds(pl.multiple_of(s * slot, slot), slot)
-        hot[:, at] = jnp.where((code & (PART - 1)) == ids, 1.0, 0.0).astype(jnp.bfloat16)
-        return c
-
-    lax.fori_loop(0, devices, mark, 0)
-
-    load_inv.wait()
-    for p in range(panels):
-        def split_inv(i, c, p=p):
-            at = pl.ds(pl.multiple_of(i * 64, 64), 64)
-            hi, lo = split(inv_f[p, at, :])
-            inv_h[p, at, :] = hi
-            inv_l[p, at, :] = lo
-            return c
-
-        lax.fori_loop(0, W // 64, split_inv, 0)
-    load_diag.wait()
-
-    def split_diag(i, c):
-        at = pl.ds(pl.multiple_of(i * 16, 16), 16)
-        hi, lo = split(diag_f[at, :])
-        diag_h[at, :] = hi
-        diag_l[at, :] = lo
-        return c
-
-    lax.fori_loop(0, rd // 16, split_diag, 0)
-
-    for p in range(panels - 1):
-        @pl.when(plane > p)
-        def _(p=p):
-            for n in range(2):
-                columns = pl.ds(n * (W // 2), W // 2)
-                left_h = diag_h[:, pl.ds(p * W, W)]
-                left_l = diag_l[:, pl.ds(p * W, W)]
-                right_h = inv_h[p, :, columns]
-                product = (jnp.dot(left_h, right_h, preferred_element_type=jnp.float32)
-                           + jnp.dot(left_l, right_h, preferred_element_type=jnp.float32)
-                           + jnp.dot(left_h, inv_l[p, :, columns], preferred_element_type=jnp.float32))
-                hi, lo = split(product)
-                step_h[p, :, columns] = hi
-                step_l[p, :, columns] = lo
-
-    load_off.wait()
-
-    def split_off(i, c):
-        at = pl.ds(pl.multiple_of(i * 16, 16), 16)
-        hi, lo = split(off_f[at, :])
-        off_h[at, :] = hi
-        off_l[at, :] = lo
-        return c
-
-    lax.fori_loop(0, od // 16, split_off, 0)
+    pl.when(jnp.logical_not(early))(prepare)
+    pl.when(plane > 0)(split_lower)
 
     group = 4
     span = group * slot
@@ -269,15 +277,41 @@
 
         lax.fori_loop(0, chunks, step, 0)
 
-    def share(to, j):
+    some = nrhs // CUTS
+
+    def share(to, j, c):
+        at = pl.ds(c * some, some)
         return pltpu.make_async_remote_copy(
-            src_ref=rhsbuf.at[j],
-            dst_ref=rhsbuf.at[j],
-            send_sem=pan_send.at[to],
-            recv_sem=pan_recv.at[j],
+            src_ref=rhsbuf.at[j, at, :],
+            dst_ref=rhsbuf.at[j, at, :],
+            send_sem=pan_send.at[to * CUTS + c],
+            recv_sem=pan_recv.at[j * CUTS + c],
             device_id=(f, to),
             device_id_type=MESH,
         )
+
+    def first_targets(p):
+        if p == panels - 1:
+            return [q * per + i for q in range(panels - 1) for i in range(per)]
+        return [(p + 1) * per + lax.rem(place + i, per) for i in range(per)]
+
+    def later_targets(p):
+        targets = [p * per + lax.rem(place + i, per) for i in range(1, per)]
+        if p < panels - 1:
+            targets += [q * per + lax.rem(place + i, per)
+                        for q in [*range(p + 2, panels), *range(p - 1, -1, -1)] for i in range(per)]
+        return targets
+
+    def offer(p, c):
+        at = pl.ds(c * some, some)
+        rhsbuf[r, at, :] = upper[at, :]
+        for to in first_targets(p):
+            share(to, r, c).start()
+
+    def offer_rest(p):
+        for to in later_targets(p):
+            for c in range(CUTS):
+                share(to, r, c).start()
 
     def finish(p, b2):
         piece = dot3(b2, inv_h[p], inv_l[p])
@@ -287,38 +321,44 @@
                 solved_ref[0] = piece[:, i * rd:(i + 1) * rd]
         off_update(p, jnp.concatenate(split(piece), axis=0))
 
+    @pl.when(plane == 0)
+    def _():
+        for c in range(CUTS):
+            offer(0, c)
+        offer_rest(0)
+
     b2 = None
     for p in range(panels):
-        @pl.when(plane == p)
-        def _(p=p):
-            rhsbuf[r] = upper[...]
-            if p < panels - 1:
-                targets = [(p + 1) * per + lax.rem(place + i, per) for i in range(per)]
-                targets += [p * per + lax.rem(place + i, per) for i in range(1, per)]
-                targets += [q * per + lax.rem(place + i, per)
-                            for q in [*range(p + 2, panels), *range(p - 1, -1, -1)] for i in range(per)]
-            else:
-                targets = [q * per + i for q in range(panels - 1) for i in range(per)]
-                targets += [p * per + lax.rem(place + i, per) for i in range(1, per)]
-            for to in targets:
-                share(to, r).start()
-
         if p == 0:
+            pl.when(plane == 0)(split_lower)
             scatter_lower()
         else:
             finish(p - 1, b2)
 
-        for j in range(p * per, (p + 1) * per):
-            @pl.when(r != j)
-            def _(j=j):
-                share(j, j).wait_recv()
-
-        b = jnp.concatenate([rhsbuf[j] for j in range(p * per, (p + 1) * per)], axis=1)
-        b2 = jnp.concatenate(split(b), axis=0)
+        owners = range(p * per, (p + 1) * per)
+        for c in range(CUTS):
+            at = pl.ds(c * some, some)
+            for j in owners:
+                @pl.when(r != j)
+                def _(j=j, c=c):
+                    share(j, j, c).wait_recv()
+
+            if p < panels - 1:
+                @pl.when(plane > p)
+                def _(p=p, at=at):
+                    part = jnp.concatenate([rhsbuf[j, at, :] for j in owners], axis=1)
+                    upper[at, :] -= dot3(jnp.concatenate(split(part), axis=0), step_h[p], step_l[p])
+
+                @pl.when(plane == p + 1)
+                def _(p=p, c=c):
+                    offer(p + 1, c)
+
         if p < panels - 1:
-            @pl.when(plane > p)
-            def _(b2=b2, p=p):
-                upper[...] -= dot3(b2, step_h[p], step_l[p])
+            @pl.when(plane == p + 1)
+            def _(p=p):
+                offer_rest(p + 1)
+
+        b2 = jnp.concatenate(split(jnp.concatenate([rhsbuf[j] for j in owners], axis=1)), axis=0)
 
     finish(panels - 1, b2)
 
@@ -334,7 +374,8 @@
     lax.fori_loop(0, devices, sent, 0)
 
     def shared(d, c):
-        share(lax.rem(r + d, nr), r).wait_send()
+        for c in range(CUTS):
+            share(lax.rem(r + d, nr), r, c).wait_send()
         return c
 
     lax.fori_loop(1, nr, shared, 0)
@@ -365,7 +406,7 @@
     )
     results = pl.pallas_call(
         functools.partial(kernel, nf, nr),
-        out_shape=outs,
+        out_shape=(pltpu.VMEM((1, nrhs, rd), f32), pltpu.VMEM((1, nrhs, od), f32)),
         in_specs=[anywhere] * 8,
         out_specs=(vmem, vmem),
         scratch_shapes=[
@@ -395,13 +436,14 @@
             pltpu.SemaphoreType.DMA,
             pltpu.SemaphoreType.DMA((devices,)),
             pltpu.SemaphoreType.DMA((devices,)),
-            pltpu.SemaphoreType.DMA((nr,)),
-            pltpu.SemaphoreType.DMA((nr,)),
+            pltpu.SemaphoreType.DMA((nr * CUTS,)),
+            pltpu.SemaphoreType.DMA((nr * CUTS,)),
         ],
         compiler_params=pltpu.CompilerParams(
             collective_id=0, has_side_effects=True, vmem_limit_bytes=58 * 1024 * 1024),
     )(rhs_diag, rhs_off, diag_factor, off_factor, diag_inverse, pattern, vals, rows)
-    return pl.pallas_call(hand_out, out_shape=outs, in_specs=[vmem, vmem], out_specs=(vmem, vmem))(*results)
+    return pl.pallas_call(hand_out, out_shape=outs, in_specs=[vmem, vmem], out_specs=(vmem, vmem),
+        compiler_params=pltpu.CompilerParams(vmem_limit_bytes=1024 * 1024))(*results)
 
 
 def solution(mesh):

time: 43.2 us -> 41.7 us (0.965)
  Pallas kernels: 42.4 us -> 40.8 us
    pallas_call x1, Pallas kernels: 1.64 us -> 0.7 us  [local(): pl.pallas_call(hand_out, out_shape=outs, in_specs=[vmem, vmem], out_specs...]
    pallas_call x1, Pallas kernels: 40.8 us -> 40.1 us  [local(): pl.pallas_call(functools.partial(kernel, nf, nr), out_shape=(pltpu.VMEM((...]
where the time goes in v2:
time: 41.7 us; the launch traced here: 41.4 us
  Pallas kernels  40.8 us (98%)
  between operations  0.64 us (2%)
    pallas_call x1, Pallas kernels, local(): pl.pallas_call(functools.partial(kernel, nf, nr), out_shape=(pltpu.VMEM((...  40.1 us

profile of v2, /device:TPU:0, one launch (start us, length us, event | category | flops | bytes accessed | tf_op | source)
XLA Modules:
  0.0 41.4 jit_solution(10331141168528600789)
XLA Ops:
  0.6 40.1 %shard_map.95 = (f32[1,32,256]{2,1,0:T(8,128)S(1)}, f32[1,32,1536]{2,1,0:T(8,128)S(1)}) custom-call(f32[1,32,256]{2,1,0:T(8,128)} %rd_hbm.1, f32[1,32,1536]{2,1,0:T(8,128)} %ro_hbm.1, f32[1,256,2048]{2,1,0:T(8,128)} %diag_hbm.1, f32[1,1536,2048]{2,1,0:T(8,128)} %off_hbm.1, f32[1,4,512,512]{3,2,1,0:T(8,128)} %inv_hbm.1, s32[1,4,12]{2,1,0:T(4,128)} %pat_hbm.1, ...), custom_call_target="tpu_custom_call" | custom-call | tf_op jit(solution)/shard_map/pallas_call | solution.py:407
  40.7 0.7 %shard_map.96 = (f32[1,32,256]{2,1,0:T(8,128)}, f32[1,32,1536]{2,1,0:T(8,128)}) custom-call(f32[1,32,256]{2,1,0:T(8,128)S(1)} %get-tuple-element.4.solved_in, f32[1,32,1536]{2,1,0:T(8,128)S(1)} %get-tuple-element.5.rem_in), custom_call_target="tpu_custom_call" | custom-call | tf_op jit(solution)/shard_map/pallas_call | solution.py:445
